TPU v7x, 32 devices: a whole 2x2x4 slice. The times are simulated.
32 devices in a mesh: dap: 8 (over z, x), head: 4 (over y, core).
Axes of the slice: x: 2, y: 2, z: 4, core: 2. Of those that a mesh axis runs over, the one named last changes fastest.
Arguments:
- multiple_aligned_family: bfloat16 [128, 128, 256], P('dap')
- homolog_present_flags: int32 [128], replicated, may hold values from 0 to 1, as said below
- amino_present_flags: int32 [128], replicated, may hold values 0 or 1
- focus_layernorm_scaling: float32 [256], replicated, may hold values from 0.5 to 1.5
- focus_layernorm_offset: float32 [256], replicated, may hold values from -1.8 to 1.8
- combined_focus_matrices: bfloat16 [256, 4, 256], P(None, None, 'head')
- sigmoid_switch_offset: float32 [256], P('head'), may hold values from -4 to 4
- focus_final_matrix: bfloat16 [256, 256], P('head'), may hold values from -0.375 to 0.375
- focus_final_offset: float32 [256], replicated, may hold values from -3 to 3
- tensor_layernorm_scaling: float32 [256], replicated, may hold values from 0.5 to 1.5
- tensor_layernorm_offset: float32 [256], replicated, may hold values from -1.8 to 1.8
- tensor_product_factors: bfloat16 [256, 2, 32], replicated, may hold values from -0.375 to 0.375
- tensor_final_matrix: float32 [1024, 128], replicated, may hold values from -0.1875 to 0.1875
- tensor_final_offset: float32 [128], replicated, may hold values from -4 to 4
Outputs:
- alignment_output: bfloat16 [128, 128, 256], P(('dap', 'head'))
- pair_mean_update: float32 [128, 128, 128], P('dap', 'head')
Inputs may be any that keep to these rules, and one draw needn't show every extreme that they name: homolog_present_flags[0] is always 1.
All inputs are finite; a program needn't handle non-finite values.
Results may differ from a plain program's by a relative error of at most 0.005.
Values may be sent and summed in bfloat16 or wider, within the bound.
A program may use at most 256 MiB of HBM per device.

v0:
```python
import jax
import jax.numpy as jnp
from jax import lax
from jax.sharding import PartitionSpec as P

DH = 32
CO = 32


def layer_norm(value, gain, bias):
    mean = jnp.mean(value, -1, keepdims=True)
    centred = value - mean
    spread = jnp.mean(centred * centred, -1, keepdims=True)
    return centred * lax.rsqrt(spread + 1e-05) * gain + bias


def attend_column(query, keys, values, gate, keep):
    scores = jnp.einsum("shd,thd->hst", query, keys, preferred_element_type=jnp.float32)
    scores = jnp.where(keep[None, None, :], scores, jnp.float32(-1000000000.0))
    top = jnp.max(scores, -1, keepdims=True)
    weights = jnp.exp(scores - top)
    probs = (weights / jnp.sum(weights, -1, keepdims=True)).astype(jnp.bfloat16)
    mixed = jnp.einsum("hst,thd->shd", probs, values, preferred_element_type=jnp.float32)
    return (mixed * gate).astype(jnp.bfloat16)


def per_device(
    multiple_aligned_family,
    homolog_present_flags,
    amino_present_flags,
    focus_layernorm_scaling,
    focus_layernorm_offset,
    combined_focus_matrices,
    sigmoid_switch_offset,
    focus_final_matrix,
    focus_final_offset,
    tensor_layernorm_scaling,
    tensor_layernorm_offset,
    tensor_product_factors,
    tensor_final_matrix,
    tensor_final_offset,
):
    parallel_devices = lax.axis_size("dap")
    n_head = lax.axis_size("head")
    head_id = lax.axis_index("head")
    dap_id = lax.axis_index("dap")
    homolog_shard_number, amino_total, feature_dimension = multiple_aligned_family.shape
    total_seqs = homolog_present_flags.shape[0]
    residue_device_count = amino_total // parallel_devices
    local_heads = sigmoid_switch_offset.shape[0] // DH
    keep = homolog_present_flags > 0
    weights_in = combined_focus_matrices.reshape(feature_dimension, 4 * local_heads * DH)
    gate_shift = sigmoid_switch_offset.reshape(local_heads, DH)
    bundled_focus_units = multiple_aligned_family.reshape(
        homolog_shard_number, parallel_devices, residue_device_count, feature_dimension
    )
    received = lax.all_to_all(bundled_focus_units, "dap", split_axis=1, concat_axis=0, tiled=True)
    block = received[:, 0]
    count = block.shape[1]
    normed = layer_norm(
        block.astype(jnp.float32), focus_layernorm_scaling, focus_layernorm_offset
    ).astype(jnp.bfloat16)
    projected = jnp.dot(
        normed.reshape(total_seqs * count, feature_dimension),
        weights_in,
        preferred_element_type=jnp.float32,
    )
    projected = projected.reshape(total_seqs, count, 4, local_heads, DH)
    query = jnp.moveaxis((projected[:, :, 0] * DH ** (-0.5)).astype(jnp.bfloat16), 1, 0)
    keys = jnp.moveaxis(projected[:, :, 1].astype(jnp.bfloat16), 1, 0)
    values = jnp.moveaxis(projected[:, :, 2].astype(jnp.bfloat16), 1, 0)
    gate = jnp.moveaxis(jax.nn.sigmoid(projected[:, :, 3] + gate_shift), 1, 0)

    def single(operands):
        return attend_column(operands[0], operands[1], operands[2], operands[3], keep)

    attended = lax.map(single, (query, keys, values, gate))
    attended = jnp.moveaxis(attended, 0, 1).reshape(total_seqs * count, local_heads * DH)
    partial_value = jnp.dot(attended, focus_final_matrix, preferred_element_type=jnp.float32)
    partial_value, columns = (
        partial_value.reshape(total_seqs, 1, count, feature_dimension),
        received,
    )
    group = homolog_shard_number // n_head
    columns = columns.reshape(
        parallel_devices, n_head, group, residue_device_count, feature_dimension
    )
    partial_value = partial_value.reshape(
        parallel_devices, n_head, group, residue_device_count, feature_dimension
    )
    summed = lax.psum(partial_value.astype(jnp.bfloat16), "head").astype(jnp.float32)
    summed_mine = lax.dynamic_index_in_dim(summed, head_id, 1, keepdims=True)
    own = lax.dynamic_index_in_dim(columns, head_id, 1, keepdims=True)
    mine = (own.astype(jnp.float32) + summed_mine + focus_final_offset).astype(jnp.bfloat16)
    alignment_rows = lax.all_to_all(
        mine.reshape(parallel_devices * group, residue_device_count, feature_dimension),
        "dap",
        split_axis=0,
        concat_axis=1,
        tiled=True,
    )
    seq_keep = homolog_present_flags.astype(jnp.float32).reshape(parallel_devices, n_head, group)
    row_keep = lax.dynamic_slice_in_dim(
        amino_present_flags, dap_id * residue_device_count, residue_device_count
    ).astype(jnp.float32)
    stack = mine.reshape(parallel_devices * group, residue_device_count, feature_dimension)
    mask_seq = lax.dynamic_index_in_dim(seq_keep, head_id, 1, keepdims=False).reshape(
        parallel_devices * group
    )
    left_weight = tensor_product_factors[:, 0]
    right_weight = tensor_product_factors[:, 1]
    used = stack.shape[0]
    opm_normed = layer_norm(
        stack.astype(jnp.float32), tensor_layernorm_scaling, tensor_layernorm_offset
    ).astype(jnp.bfloat16)
    flat = opm_normed.reshape(used * residue_device_count, feature_dimension)
    keep_rs = mask_seq[:, None, None] * row_keep[None, :, None]
    left = (
        jnp.dot(flat, left_weight, preferred_element_type=jnp.float32).reshape(
            used, residue_device_count, -1
        )
        * keep_rs
    ).astype(jnp.bfloat16)
    right = (
        jnp.dot(flat, right_weight, preferred_element_type=jnp.float32).reshape(
            used, residue_device_count, CO
        )
        * keep_rs
    ).astype(jnp.bfloat16)
    piece = lax.all_gather(right, "dap", axis=1, tiled=True)
    outer = lax.dot_general(
        left, piece, (((0,), (0,)), ((), ())), preferred_element_type=jnp.float32
    )
    outer = outer.transpose(0, 2, 1, 3).reshape(residue_device_count, piece.shape[1], -1)
    partial_pair = jnp.dot(
        outer,
        tensor_final_matrix,
        precision=lax.Precision.HIGHEST,
        preferred_element_type=jnp.float32,
    )
    pair = lax.psum_scatter(partial_pair, "head", scatter_dimension=1, tiled=True)
    col_width = amino_total // n_head
    col_keep = lax.dynamic_slice_in_dim(amino_present_flags, head_id * col_width, col_width).astype(
        jnp.float32
    )
    count = jnp.sum(homolog_present_flags).astype(jnp.float32)
    norm = jnp.maximum(count * row_keep[:, None] * col_keep[None, :], 1.0)
    pair_mean_update = (pair + tensor_final_offset) / norm[:, :, None]
    return (alignment_rows, pair_mean_update)


def solution(mesh):
    return jax.shard_map(
        per_device,
        mesh=mesh,
        in_specs=(
            P("dap", None, None),
            P(),
            P(),
            P(),
            P(),
            P(None, None, "head"),
            P("head"),
            P("head", None),
            P(),
            P(),
            P(),
            P(),
            P(),
            P(),
        ),
        out_specs=(P(("dap", "head"), None, None), P("dap", "head", None)),
        check_vma=False,
    )
```

profile of v0, /device:TPU:0, one launch (start us, length us, event | category | flops | bytes accessed | tf_op | source)
XLA Modules:
  0.0 189.5 jit_solution(11915135432507252343)
XLA Ops:
  7.2 2.4 %copy.23 = bf16[16,8,16,256]{3,2,0,1:T(8,128)(2,1)} copy(bf16[16,8,16,256]{3,2,1,0:T(8,128)(2,1)} %bitcast.152) | data formatting | bytes 2097152 | tf_op jit(solution)/shard_map/reshape | solution.py:54
  9.6 7.4 %all-to-all-start = ((bf16[16,8,16,256]{3,2,0,1:T(8,128)(2,1)}), bf16[16,8,16,256]{3,2,0,1:T(8,128)(2,1)S(1)}, u32[]{:S(2)}, u32[]{:S(2)}) async-start(bf16[16,8,16,256]{3,2,0,1:T(8,128)(2,1)} %copy.23), calls=%async_computation | async-start | bytes 2097152 | tf_op jit(solution)/shard_map/all_to_all | solution.py:57
  17.1 25.6 %all-to-all-done = bf16[16,8,16,256]{3,2,0,1:T(8,128)(2,1)S(1)} async-done(((bf16[16,8,16,256]{3,2,0,1:T(8,128)(2,1)}), bf16[16,8,16,256]{3,2,0,1:T(8,128)(2,1)S(1)}, u32[]{:S(2)}, u32[]{:S(2)}) %all-to-all-start) | async-done | bytes 1048608 | tf_op jit(solution)/shard_map/all_to_all | solution.py:57
  42.8 0.3 convert_reduce_fusion
  43.1 0.7 fusion.43
  43.8 0.7 fusion.46
  44.6 0.3 copy.24
  44.9 0.5 fusion.79
  45.5 0.2 fusion.59
  45.8 10.6 %while.10 = (s32[]{:T(128)}, bf16[16,128,2,32]{1,3,2,0:T(8,128)(2,1)S(1)}, bf16[16,128,2,32]{1,3,2,0:T(8,128)(2,1)S(1)}, pred[128]{0:T(512)(128)(4,1)S(1)}, bf16...) while((s32[]{:T(128)}, ...), condition=%wide.region_5.6_spmd, body=%wide.region_2.5_spmd.sunk | while | flops 6537728 | bytes 137301 | solution.py:77
  45.8 0.3 fusion.98
  46.0 0.4 fusion.99
  46.4 0.3 fusion.98
  46.7 0.4 fusion.99
  47.1 0.3 fusion.98
  47.4 0.4 fusion.99
  47.8 0.3 fusion.98
  48.0 0.4 fusion.99
  48.4 0.3 fusion.98
  48.7 0.4 fusion.99
  49.1 0.3 fusion.98
  49.4 0.4 fusion.99
  49.7 0.3 fusion.98
  50.0 0.4 fusion.99
  50.4 0.3 fusion.98
  50.7 0.4 fusion.99
  51.1 0.3 fusion.98
  51.3 0.4 fusion.99
  51.7 0.3 fusion.98
  52.0 0.4 fusion.99
  52.4 0.3 fusion.98
  52.7 0.4 fusion.99
  53.1 0.3 fusion.98
  53.3 0.4 fusion.99
  53.7 0.3 fusion.98
  54.0 0.4 fusion.99
  54.4 0.3 fusion.98
  54.7 0.4 fusion.99
  55.0 0.3 fusion.98
  55.3 0.4 fusion.99
  55.7 0.3 fusion.98
  56.0 0.4 fusion.99
  56.4 0.9 copy.25
  57.3 0.5 dot_general.33
  57.9 1.4 convolution_convert_fusion
  59.4 0.6 fusion.78
  60.0 0.1 reshape.285
  61.1 33.8 %all-reduce.2.cloned.1.call-done = bf16[8,4,4,16,256]{4,3,2,1,0:T(8,128)(2,1)} async-done(((bf16[8,4,4,16,256]{4,3,2,1,0:T(8,128)(2,1)}), bf16[8,4,4,16,256]{4,3,2,1,0:T(8,128)(2,1)}) %all-reduce.2.cloned.1.call-update) | async-done | bytes 1048592 | tf_op jit(solution)/shard_map/psum | solution.py:91
  94.8 1.7 convert_reduce_fusion.1
  96.6 1.2 fusion.50
  97.9 1.2 fusion.53
  99.0 0.2 fusion.69
  99.2 0.2 fusion.67
  99.4 0.2 copy.33
  99.6 0.2 copy.34
  99.9 33.2 %all_gather.3 = bf16[32,128,32]{0,1,2:T(8,128)(2,1)S(1)} all-gather(bf16[32,16,32]{0,1,2:T(8,128)(2,1)S(1)} %get-tuple-element.61), channel_id=1, replica_groups=mesh['dap'=8,'head'=4] {'dap'}, dimensions={1}, use_global_device_ids=true | all-gather | bytes 294912 | tf_op jit(solution)/shard_map/all_gather | solution.py:130
  133.1 1.3 convolution_bitcast_fusion.1
  134.3 6.5 %copy.28 = f32[16,128,32,32]{1,3,2,0:T(8,128)S(1)} copy(f32[16,128,32,32]{1,2,3,0:T(8,128)S(1)} %convolution_bitcast_fusion.1) | data formatting | bytes 16777216 | tf_op jit(solution)/shard_map/transpose | solution.py:134
  140.8 14.9 %fusion.61 = f32[16,128,128]{2,1,0:T(8,128)} fusion(f32[16,128,1024]{1,2,0:T(8,128)S(1)} %bitcast.147, f32[1024,128]{1,0:T(8,128)S(1)} %copy-done), kind=kOutput, calls=%fused_computation.52 | convolution fusion | flops 3221225472 | bytes 9961472 | tf_op jit(solution)/shard_map/dot_general | solution.py:135
  155.7 5.4 %all-to-all-start.1 = ((bf16[32,16,256]{2,1,0:T(8,128)(2,1)}), bf16[32,16,256]{2,1,0:T(8,128)(2,1)S(1)}, u32[]{:S(2)}, u32[]{:S(2)}) async-start(bf16[32,16,256]{2,1,0:T(8,128)(2,1)} %bitcast.29), calls=%async_computation.1 | async-start | bytes 524288 | tf_op jit(solution)/shard_map/all_to_all | solution.py:95
  161.2 8.1 %all-to-all-done.1 = bf16[32,16,256]{2,1,0:T(8,128)(2,1)S(1)} async-done(((bf16[32,16,256]{2,1,0:T(8,128)(2,1)}), bf16[32,16,256]{2,1,0:T(8,128)(2,1)S(1)}, u32[]{:S(2)}, u32[]{:S(2)}) %all-to-all-start.1) | async-done | bytes 262176 | tf_op jit(solution)/shard_map/all_to_all | solution.py:95
  169.3 0.7 copy.26
  170.0 10.8 %reduce-scatter.2.cloned.1.call-done = f32[16,32,128]{2,1,0:T(8,128)} async-done(((f32[16,128,128]{2,1,0:T(8,128)}), f32[16,32,128]{2,1,0:T(8,128)}) %reduce-scatter.2.cloned.1.call-update) | async-done | bytes 262160 | tf_op jit(solution)/shard_map/reduce_scatter | solution.py:141
  180.8 1.8 add_divide_fusion
  (46 shorter events, 0.9 us)
Async XLA Ops:
  7.2 133.6 %copy-start = (f32[1024,128]{1,0:T(8,128)S(1)}, f32[1024,128]{1,0:T(8,128)}, u32[]{:S(2)}) copy-start(f32[1024,128]{1,0:T(8,128)} %param.28) | copy-start | bytes 1572868
  7.2 9.9 %copy-start.11 = (f32[64]{0:T(128)S(1)}, f32[64]{0:T(128)}, u32[]{:S(2)}) copy-start(f32[64]{0:T(128)} %param.22) | copy-start | bytes 772
  7.2 9.9 %copy-start.12 = (s32[128]{0:T(128)S(1)}, s32[128]{0:T(128)}, u32[]{:S(2)}) copy-start(s32[128]{0:T(128)} %param.17) | copy-start | bytes 1540
  9.6 34.2 %copy-start.4 = (f32[256]{0:T(256)S(1)}, f32[256]{0:T(256)}, u32[]{:S(2)}) copy-start(f32[256]{0:T(256)} %param.20) | copy-start | bytes 3076
  9.6 34.2 %copy-start.5 = (f32[256]{0:T(256)S(1)}, f32[256]{0:T(256)}, u32[]{:S(2)}) copy-start(f32[256]{0:T(256)} %param.19) | copy-start | bytes 3076
  9.6 33.2 %all-to-all-start = ((bf16[16,8,16,256]{3,2,0,1:T(8,128)(2,1)}), bf16[16,8,16,256]{3,2,0,1:T(8,128)(2,1)S(1)}, u32[]{:S(2)}, u32[]{:S(2)}) async-start(bf16[16,8,16,256]{3,2,0,1:T(8,128)(2,1)} %copy.23), calls=%async_computation | async-start | bytes 2097152 | tf_op jit(solution)/shard_map/all_to_all | solution.py:57
  17.0 77.9 %all-reduce.2.cloned.1.call-start = ((), (), s32[]{:S(2)}) async-start(), calls=%async_computation.3 | async-start | bytes 2097152 | tf_op jit(solution)/shard_map/psum | solution.py:91
  43.8 1.1 copy-start.1
  56.4 1.5 copy-start.2
  57.3 3.6 %copy-start.10 = (s32[128]{0:T(128)S(1)}, s32[128]{0:T(128)}, u32[]{:S(2)}) copy-start(s32[128]{0:T(128)} %param.18) | copy-start | bytes 1540
  57.3 37.5 %copy-start.6 = (f32[256]{0:T(256)S(1)}, f32[256]{0:T(256)}, u32[]{:S(2)}) copy-start(f32[256]{0:T(256)} %param.24) | copy-start | bytes 3076
  57.8 40.0 %copy-start.7 = (f32[256]{0:T(256)S(1)}, f32[256]{0:T(256)}, u32[]{:S(2)}) copy-start(f32[256]{0:T(256)} %param.26) | copy-start | bytes 3076
  57.9 40.0 %copy-start.8 = (f32[256]{0:T(256)S(1)}, f32[256]{0:T(256)}, u32[]{:S(2)}) copy-start(f32[256]{0:T(256)} %param.25) | copy-start | bytes 3076
  57.9 41.2 %copy-start.3 = (bf16[256,2,32]{0,2,1:T(8,128)(2,1)S(1)}, bf16[256,2,32]{0,2,1:T(8,128)(2,1)}, u32[]{:S(2)}) copy-start(bf16[256,2,32]{0,2,1:T(8,128)(2,1)} %param.27) | copy-start | bytes 98308
  59.3 121.5 %reduce-scatter.2.cloned.1.call-start = ((), (), s32[]{:S(2)}) async-start(), calls=%async_computation.4 | async-start | bytes 1310720 | tf_op jit(solution)/shard_map/reduce_scatter | solution.py:141
  155.7 25.1 %copy-start.9 = (f32[128]{0:T(128)S(1)}, f32[128]{0:T(128)}, u32[]{:S(2)}) copy-start(f32[128]{0:T(128)} %param.29) | copy-start | bytes 1540
  155.7 13.6 %all-to-all-start.1 = ((bf16[32,16,256]{2,1,0:T(8,128)(2,1)}), bf16[32,16,256]{2,1,0:T(8,128)(2,1)S(1)}, u32[]{:S(2)}, u32[]{:S(2)}) async-start(bf16[32,16,256]{2,1,0:T(8,128)(2,1)} %bitcast.29), calls=%async_computation.1 | async-start | bytes 524288 | tf_op jit(solution)/shard_map/all_to_all | solution.py:95
Sparse Core Ops, SparseCore 0:
  59.5 35.3 all-reduce.1
  155.9 24.9 reduce-scatter.1
where the time goes:
time: 190 us; the launch traced here: 189 us
  waiting for transfers between devices  78.3 us (41%)
  blocking collectives  33.2 us (17%)
  matrix products  29 us (15%)
  between operations  15.1 us (8%)
  starting transfers between devices  12.8 us (7%)
  local copies, waits for them, and re-layouts  12.1 us (6%)
  other arithmetic  8.95 us (5%)
    psum x1, waiting for transfers between devices, per_device(): lax.psum(partial_value.astype(jnp.bfloat16), 'head').astype(jnp.float32)  33.8 us
    all_gather x1, blocking collectives, per_device(): piece = lax.all_gather(right, 'dap', axis=1, tiled=True)  33.2 us
    all_to_all x1, waiting for transfers between devices, per_device(): lax.all_to_all(bundled_focus_units, 'dap', split_axis=1, concat_axis=0, t...  25.6 us
    dot_general x1, matrix products, per_device(): jnp.dot(outer, tensor_final_matrix, precision=lax.Precision.HIGHEST, pref...  14.9 us
    reduce_scatter x1, waiting for transfers between devices, per_device(): lax.psum_scatter(partial_pair, 'head', scatter_dimension=1, tiled=True)  10.8 us
    all_to_all x1, waiting for transfers between devices, per_device(): lax.all_to_all(mine.reshape(parallel_devices * group, residue_device_coun...  8.07 us
    all_to_all x1, starting transfers between devices, per_device(): lax.all_to_all(bundled_focus_units, 'dap', split_axis=1, concat_axis=0, t...  7.41 us
    transpose x1, local copies, waits for them, and re-layouts, per_device(): outer.transpose(0, 2, 1, 3)  6.49 us
  transfers between devices with their start and end apart: 4, of which 4 were waited for; matrix products, arithmetic and copies ran while one was open for 1% of the time, Pallas kernels for 0%

commit v1 on v0

--- a/solution.py
+++ b/solution.py
@@ -127,7 +127,7 @@
         )
         * keep_rs
     ).astype(jnp.bfloat16)
-    piece = lax.all_gather(right, "dap", axis=1, tiled=True)
+    piece = jnp.concatenate(lax.all_gather(right, "dap"), axis=1)
     outer = lax.dot_general(
         left, piece, (((0,), (0,)), ((), ())), preferred_element_type=jnp.float32
     )

time: 190 us -> 190 us (level)
  no operation moved by 1% of the time
where the time goes in v1:
time: 190 us
  waiting for transfers between devices  78.2 us (41%)
  blocking collectives  33.3 us (18%)
  matrix products  29.1 us (15%)
  between operations  15 us (8%)
  starting transfers between devices  12.7 us (7%)
  local copies, waits for them, and re-layouts  12.6 us (7%)
  other arithmetic  8.91 us (5%)
    psum x1, waiting for transfers between devices, per_device(): lax.psum(partial_value.astype(jnp.bfloat16), 'head').astype(jnp.float32)  33.8 us
    all_gather x1, blocking collectives, per_device(): piece = jnp.concatenate(lax.all_gather(right, 'dap'), axis=1)  33.3 us
    all_to_all x1, waiting for transfers between devices, per_device(): lax.all_to_all(bundled_focus_units, 'dap', split_axis=1, concat_axis=0, t...  25.6 us
    dot_general x1, matrix products, per_device(): jnp.dot(outer, tensor_final_matrix, precision=lax.Precision.HIGHEST, pref...  14.9 us
    reduce_scatter x1, waiting for transfers between devices, per_device(): lax.psum_scatter(partial_pair, 'head', scatter_dimension=1, tiled=True)  10.8 us
    all_to_all x1, waiting for transfers between devices, per_device(): lax.all_to_all(mine.reshape(parallel_devices * group, residue_device_coun...  8.07 us
    all_to_all x1, starting transfers between devices, per_device(): lax.all_to_all(bundled_focus_units, 'dap', split_axis=1, concat_axis=0, t...  7.41 us
    transpose x1, local copies, waits for them, and re-layouts, per_device(): outer.transpose(0, 2, 1, 3)  6.49 us
  transfers between devices with their start and end apart: 4, of which 4 were waited for; matrix products, arithmetic and copies ran while one was open for 1% of the time, Pallas kernels for 0%

profile of v1, /device:TPU:0, one launch (start us, length us, event | category | flops | bytes accessed | tf_op | source)
XLA Modules:
  0.0 189.9 jit_solution(5964433869791180840)
XLA Ops:
  7.2 2.4 %copy.34 = bf16[16,8,16,256]{3,2,0,1:T(8,128)(2,1)} copy(bf16[16,8,16,256]{3,2,1,0:T(8,128)(2,1)} %bitcast.158) | data formatting | bytes 2097152 | tf_op jit(solution)/shard_map/reshape | solution.py:54
  9.6 7.4 %all-to-all-start = ((bf16[16,8,16,256]{3,2,0,1:T(8,128)(2,1)}), bf16[16,8,16,256]{3,2,0,1:T(8,128)(2,1)S(1)}, u32[]{:S(2)}, u32[]{:S(2)}) async-start(bf16[16,8,16,256]{3,2,0,1:T(8,128)(2,1)} %copy.34), calls=%async_computation | async-start | bytes 2097152 | tf_op jit(solution)/shard_map/all_to_all | solution.py:57
  17.1 25.6 %all-to-all-done = bf16[16,8,16,256]{3,2,0,1:T(8,128)(2,1)S(1)} async-done(((bf16[16,8,16,256]{3,2,0,1:T(8,128)(2,1)}), bf16[16,8,16,256]{3,2,0,1:T(8,128)(2,1)S(1)}, u32[]{:S(2)}, u32[]{:S(2)}) %all-to-all-start) | async-done | bytes 1048608 | tf_op jit(solution)/shard_map/all_to_all | solution.py:57
  42.8 0.3 convert_reduce_fusion
  43.1 0.7 fusion.43
  43.8 0.7 fusion.46
  44.6 0.3 copy.35
  44.9 0.5 fusion.79
  45.5 0.2 fusion.61
  45.8 10.6 %while.10 = (s32[]{:T(128)}, bf16[16,128,2,32]{1,3,2,0:T(8,128)(2,1)S(1)}, bf16[16,128,2,32]{1,3,2,0:T(8,128)(2,1)S(1)}, pred[128]{0:T(512)(128)(4,1)S(1)}, bf16...) while((s32[]{:T(128)}, ...), condition=%wide.region_5.6_spmd, body=%wide.region_2.5_spmd.sunk | while | flops 6537728 | bytes 137301 | solution.py:77
  45.8 0.3 fusion.98
  46.0 0.4 fusion.99
  46.4 0.3 fusion.98
  46.7 0.4 fusion.99
  47.1 0.3 fusion.98
  47.4 0.4 fusion.99
  47.8 0.3 fusion.98
  48.0 0.4 fusion.99
  48.4 0.3 fusion.98
  48.7 0.4 fusion.99
  49.1 0.3 fusion.98
  49.4 0.4 fusion.99
  49.7 0.3 fusion.98
  50.0 0.4 fusion.99
  50.4 0.3 fusion.98
  50.7 0.4 fusion.99
  51.1 0.3 fusion.98
  51.3 0.4 fusion.99
  51.7 0.3 fusion.98
  52.0 0.4 fusion.99
  52.4 0.3 fusion.98
  52.7 0.4 fusion.99
  53.1 0.3 fusion.98
  53.3 0.4 fusion.99
  53.7 0.3 fusion.98
  54.0 0.4 fusion.99
  54.4 0.3 fusion.98
  54.7 0.4 fusion.99
  55.0 0.3 fusion.98
  55.3 0.4 fusion.99
  55.7 0.3 fusion.98
  56.0 0.4 fusion.99
  56.4 0.9 copy.36
  57.3 0.5 dot_general.33
  57.9 1.4 convolution_convert_fusion
  59.4 0.6 fusion.78
  60.0 0.1 reshape.291
  61.1 33.8 %all-reduce.2.cloned.1.call-done = bf16[8,4,4,16,256]{4,3,2,1,0:T(8,128)(2,1)} async-done(((bf16[8,4,4,16,256]{4,3,2,1,0:T(8,128)(2,1)}), bf16[8,4,4,16,256]{4,3,2,1,0:T(8,128)(2,1)}) %all-reduce.2.cloned.1.call-update) | async-done | bytes 1048592 | tf_op jit(solution)/shard_map/psum | solution.py:91
  94.8 1.7 convert_reduce_fusion.1
  96.6 1.2 fusion.52
  97.9 1.2 fusion.55
  99.0 0.2 fusion.48
  99.2 0.2 fusion.49
  99.5 33.3 %all-gather = bf16[256,16,32]{2,1,0:T(8,128)(2,1)S(1)} all-gather(bf16[32,16,32]{2,1,0:T(8,128)(2,1)S(1)} %fusion.48), channel_id=2, replica_groups=mesh['dap'=8,'head'=4] {'dap'}, dimensions={0}, use_global_device_ids=true | all-gather | bytes 294912 | tf_op jit(solution)/shard_map/all_gather | solution.py:130
  132.8 0.3 copy.38
  133.1 0.5 copy.40
  133.7 1.3 convolution_bitcast_fusion.1
  134.9 6.5 %copy.41 = f32[16,128,32,32]{1,3,2,0:T(8,128)S(1)} copy(f32[16,128,32,32]{1,2,3,0:T(8,128)S(1)} %convolution_bitcast_fusion.1) | data formatting | bytes 16777216 | tf_op jit(solution)/shard_map/transpose | solution.py:134
  141.4 14.9 %fusion.63 = f32[16,128,128]{2,1,0:T(8,128)} fusion(f32[16,128,1024]{1,2,0:T(8,128)S(1)} %bitcast.151, f32[1024,128]{1,0:T(8,128)S(1)} %copy-done), kind=kOutput, calls=%fused_computation.56 | convolution fusion | flops 3221225472 | bytes 9961472 | tf_op jit(solution)/shard_map/dot_general | solution.py:135
  156.4 5.2 %all-to-all-start.1 = ((bf16[32,16,256]{2,1,0:T(8,128)(2,1)}), bf16[32,16,256]{2,1,0:T(8,128)(2,1)S(1)}, u32[]{:S(2)}, u32[]{:S(2)}) async-start(bf16[32,16,256]{2,1,0:T(8,128)(2,1)} %bitcast.29), calls=%async_computation.1 | async-start | bytes 524288 | tf_op jit(solution)/shard_map/all_to_all | solution.py:95
  161.7 8.1 %all-to-all-done.1 = bf16[32,16,256]{2,1,0:T(8,128)(2,1)S(1)} async-done(((bf16[32,16,256]{2,1,0:T(8,128)(2,1)}), bf16[32,16,256]{2,1,0:T(8,128)(2,1)S(1)}, u32[]{:S(2)}, u32[]{:S(2)}) %all-to-all-start.1) | async-done | bytes 262176 | tf_op jit(solution)/shard_map/all_to_all | solution.py:95
  169.8 0.7 copy.37
  170.5 10.8 %reduce-scatter.2.cloned.1.call-done = f32[16,32,128]{2,1,0:T(8,128)} async-done(((f32[16,128,128]{2,1,0:T(8,128)}), f32[16,32,128]{2,1,0:T(8,128)}) %reduce-scatter.2.cloned.1.call-update) | async-done | bytes 262160 | tf_op jit(solution)/shard_map/reduce_scatter | solution.py:141
  181.3 1.8 add_divide_fusion
  (45 shorter events, 0.8 us)
Async XLA Ops:
  7.2 134.3 %copy-start = (f32[1024,128]{1,0:T(8,128)S(1)}, f32[1024,128]{1,0:T(8,128)}, u32[]{:S(2)}) copy-start(f32[1024,128]{1,0:T(8,128)} %param.28) | copy-start | bytes 1572868
  7.2 9.9 %copy-start.11 = (f32[64]{0:T(128)S(1)}, f32[64]{0:T(128)}, u32[]{:S(2)}) copy-start(f32[64]{0:T(128)} %param.22) | copy-start | bytes 772
  7.2 9.9 %copy-start.12 = (s32[128]{0:T(128)S(1)}, s32[128]{0:T(128)}, u32[]{:S(2)}) copy-start(s32[128]{0:T(128)} %param.17) | copy-start | bytes 1540
  9.6 34.2 %copy-start.4 = (f32[256]{0:T(256)S(1)}, f32[256]{0:T(256)}, u32[]{:S(2)}) copy-start(f32[256]{0:T(256)} %param.20) | copy-start | bytes 3076
  9.6 34.2 %copy-start.5 = (f32[256]{0:T(256)S(1)}, f32[256]{0:T(256)}, u32[]{:S(2)}) copy-start(f32[256]{0:T(256)} %param.19) | copy-start | bytes 3076
  9.6 33.2 %all-to-all-start = ((bf16[16,8,16,256]{3,2,0,1:T(8,128)(2,1)}), bf16[16,8,16,256]{3,2,0,1:T(8,128)(2,1)S(1)}, u32[]{:S(2)}, u32[]{:S(2)}) async-start(bf16[16,8,16,256]{3,2,0,1:T(8,128)(2,1)} %copy.34), calls=%async_computation | async-start | bytes 2097152 | tf_op jit(solution)/shard_map/all_to_all | solution.py:57
  17.0 77.9 %all-reduce.2.cloned.1.call-start = ((), (), s32[]{:S(2)}) async-start(), calls=%async_computation.3 | async-start | bytes 2097152 | tf_op jit(solution)/shard_map/psum | solution.py:91
  43.8 1.1 copy-start.1
  56.4 1.5 copy-start.2
  57.3 3.6 %copy-start.10 = (s32[128]{0:T(128)S(1)}, s32[128]{0:T(128)}, u32[]{:S(2)}) copy-start(s32[128]{0:T(128)} %param.18) | copy-start | bytes 1540
  57.3 37.5 %copy-start.6 = (f32[256]{0:T(256)S(1)}, f32[256]{0:T(256)}, u32[]{:S(2)}) copy-start(f32[256]{0:T(256)} %param.24) | copy-start | bytes 3076
  57.8 40.0 %copy-start.7 = (f32[256]{0:T(256)S(1)}, f32[256]{0:T(256)}, u32[]{:S(2)}) copy-start(f32[256]{0:T(256)} %param.26) | copy-start | bytes 3076
  57.9 40.0 %copy-start.8 = (f32[256]{0:T(256)S(1)}, f32[256]{0:T(256)}, u32[]{:S(2)}) copy-start(f32[256]{0:T(256)} %param.25) | copy-start | bytes 3076
  57.9 41.2 %copy-start.3 = (bf16[256,2,32]{0,2,1:T(8,128)(2,1)S(1)}, bf16[256,2,32]{0,2,1:T(8,128)(2,1)}, u32[]{:S(2)}) copy-start(bf16[256,2,32]{0,2,1:T(8,128)(2,1)} %param.27) | copy-start | bytes 98308
  59.3 121.9 %reduce-scatter.2.cloned.1.call-start = ((), (), s32[]{:S(2)}) async-start(), calls=%async_computation.4 | async-start | bytes 1310720 | tf_op jit(solution)/shard_map/reduce_scatter | solution.py:141
  156.3 24.9 %copy-start.9 = (f32[128]{0:T(128)S(1)}, f32[128]{0:T(128)}, u32[]{:S(2)}) copy-start(f32[128]{0:T(128)} %param.29) | copy-start | bytes 1540
  156.4 13.4 %all-to-all-start.1 = ((bf16[32,16,256]{2,1,0:T(8,128)(2,1)}), bf16[32,16,256]{2,1,0:T(8,128)(2,1)S(1)}, u32[]{:S(2)}, u32[]{:S(2)}) async-start(bf16[32,16,256]{2,1,0:T(8,128)(2,1)} %bitcast.29), calls=%async_computation.1 | async-start | bytes 524288 | tf_op jit(solution)/shard_map/all_to_all | solution.py:95
Sparse Core Ops, SparseCore 0:
  59.5 35.3 all-reduce.1
  156.5 24.7 reduce-scatter.1
